TPU v7x, 256 devices: a whole 4x4x8 slice. The times are simulated.
256 devices in a mesh: pw: 64 (over y_lo, z, x), atom: 4 (over y_hi, core).
Axes of the slice: x: 4, y: 4 (y_hi: 2, y_lo: 2; y = y_hi * 2 + y_lo), z: 8, core: 2. Of those that a mesh axis runs over, the one named last changes fastest.
Arguments:
- bands_in: float32 [2, 8, 32768], P(None, None, 'pw'), may hold values from -6 to 6
- template: bfloat16 [2, 64, 32768], P(None, None, 'pw'), may hold values from -0.03125 to 0.03125
- potential: bfloat16 [1024, 8192], P(('pw', 'atom')), may hold values from -0.5 to 0.5
- miller: int32 [3, 32768], P(None, 'pw'), may hold values from -32 to 32, as said below
- positions: float32 [3, 1024], replicated, may hold values from 0 to 1
- species: int32 [1024], replicated, may hold values from 0 to 1
- atom_order: int32 [1024], replicated, may hold values from 0 to 1023, each once
- reciprocal: float32 [3], replicated, may hold values from 0.03 to 0.1
Outputs:
- applied_once: float32 [2, 8, 32768], P(None, None, 'pw')
- applied_twice: float32 [2, 8, 32768], P(None, None, 'pw')
Inputs may be any that keep to these rules, and one draw needn't show every extreme that they name: `atom_order`: each atom stands in exactly one slot. `miller`: no two plane waves have the same triple of Miller indices; the triples (-32, -32, -32) and (32, 32, 32) are always among them.
All inputs are finite; a program needn't handle non-finite values.
Results may differ from a plain program's by a relative error of at most 0.005.
Values may be sent and summed in bfloat16 or wider, within the bound.
No kernel may reach another device: no remote copies, remote signals or barrier semaphores. Data moves between devices by JAX's collectives and lax.ppermute only.
A program may use at most 64 MiB of HBM per device.

v0:
```python
import math
import jax
import jax.numpy as jnp
from jax import lax
from jax.sharding import PartitionSpec as P

full_turn = 2.0 * math.pi


def phases(miller_real, centres):
    angles = full_turn * (
        centres[0][:, None] * miller_real[0][None, :]
        + centres[1][:, None] * miller_real[1][None, :]
        + centres[2][:, None] * miller_real[2][None, :]
    )
    return (jnp.cos(angles), jnp.sin(angles))


def project_block(template_flat, fields, cos_part, sin_part, chosen):
    band_count = fields.shape[1]
    real_wave = cos_part[:, None, :] * fields[0][None] - sin_part[:, None, :] * fields[1][None]
    imag_wave = sin_part[:, None, :] * fields[0][None] + cos_part[:, None, :] * fields[1][None]
    stacked = jnp.stack([real_wave, imag_wave], axis=1).astype(jnp.bfloat16)
    atom_count = stacked.shape[0]
    flattened = stacked.reshape(atom_count * 2 * band_count, stacked.shape[3])
    correlations = lax.dot_general(
        template_flat, flattened, (((1,), (1,)), ((), ())), preferred_element_type=jnp.float32
    )
    species_count = chosen.shape[1]
    harmonics = template_flat.shape[0] // species_count
    correlations = correlations.reshape(species_count, harmonics, atom_count, 2, band_count)
    accumulated = jnp.zeros((harmonics, atom_count, 2, band_count), jnp.float32)
    for species_id in range(species_count):
        accumulated = (
            accumulated + chosen[:, species_id][None, :, None, None] * correlations[species_id]
        )
    return jnp.transpose(accumulated, (1, 2, 0, 3))


def product(matrices, vectors):
    return jnp.einsum("alm,amb->alb", matrices, vectors, precision=lax.Precision.HIGHEST)


def apply_potential(potential, coeffs):
    atom_count = coeffs.shape[0]
    harmonics = coeffs.shape[2]
    matrices = potential.astype(jnp.float32).reshape(atom_count, 2, harmonics, harmonics)
    real_new = product(matrices[:, 0], coeffs[:, 0]) - product(matrices[:, 1], coeffs[:, 1])
    imag_new = product(matrices[:, 0], coeffs[:, 1]) + product(matrices[:, 1], coeffs[:, 0])
    return jnp.stack([real_new, imag_new], axis=1).astype(jnp.bfloat16)


def return_block(template_flat, applied, cos_part, sin_part, chosen):
    atom_count, _, harmonics, band_count = applied.shape
    species_count = chosen.shape[1]
    reordered = jnp.transpose(applied, (2, 0, 1, 3))
    selected = jnp.stack(
        [
            reordered * chosen[:, species_id][None, :, None, None].astype(jnp.bfloat16)
            for species_id in range(species_count)
        ]
    )
    selected = selected.reshape(species_count * harmonics, atom_count * 2 * band_count)
    images = lax.dot_general(
        selected, template_flat, (((0,), (0,)), ((), ())), preferred_element_type=jnp.float32
    )
    images = images.reshape(atom_count, 2, band_count, template_flat.shape[1])
    real_out = jnp.sum(
        cos_part[:, None, :] * images[:, 0] + sin_part[:, None, :] * images[:, 1], axis=0
    )
    imag_out = jnp.sum(
        cos_part[:, None, :] * images[:, 1] - sin_part[:, None, :] * images[:, 0], axis=0
    )
    return jnp.stack([real_out, imag_out])


def per_device(bands_in, template, potential, miller, positions, species, atom_order, reciprocal):
    pw_count = lax.axis_size("pw")
    group_count = lax.axis_size("atom")
    group_id = lax.axis_index("atom")
    slot_dev = potential.shape[0]
    per_group = slot_dev * pw_count
    species_count, harmonics, wave_count = template.shape
    band_count = bands_in.shape[1]
    template_flat = template.reshape(species_count * harmonics, wave_count)
    local_rows = jnp.arange(per_group, dtype=jnp.int32)
    slot_ids = (local_rows // slot_dev * group_count + group_id) * slot_dev + local_rows % slot_dev
    atoms_here = atom_order[slot_ids]
    centres = positions[:, atoms_here]
    kinds = species[atoms_here]
    chosen = (kinds[:, None] == jnp.arange(species_count, dtype=jnp.int32)[None, :]).astype(
        jnp.float32
    )
    miller_real = miller.astype(jnp.float32)
    kinetic = 0.5 * (
        (reciprocal[0] * miller_real[0]) ** 2
        + (reciprocal[1] * miller_real[1]) ** 2
        + (reciprocal[2] * miller_real[2]) ** 2
    )
    cos_all, sin_all = phases(miller_real, centres)
    block_size = math.gcd(per_group, 32)
    block_count = per_group // block_size
    row_width = 2 * harmonics * band_count

    def apply_once(fields):

        def projected(blocknum):
            first_row = blocknum * block_size
            chosen_part = lax.dynamic_slice_in_dim(chosen, first_row, block_size, 0)
            cos_part = lax.dynamic_slice_in_dim(cos_all, first_row, block_size, 0)
            sin_part = lax.dynamic_slice_in_dim(sin_all, first_row, block_size, 0)
            return project_block(template_flat, fields, cos_part, sin_part, chosen_part)

        coeffs = lax.map(projected, jnp.arange(block_count, dtype=jnp.int32)).reshape(
            per_group, row_width
        )
        summed = lax.psum(coeffs, "pw")
        segment = lax.all_gather(potential, "pw", axis=0, tiled=True)
        row_count = segment.shape[0]
        segment_coeffs = summed.reshape(row_count, 2, harmonics, band_count)
        applied = apply_potential(segment, segment_coeffs).reshape(row_count, row_width)
        applied = applied.reshape(per_group, 2, harmonics, band_count)

        def returned(blocknum, summed_up):
            first_row = (blocknum * block_size).astype(jnp.int32)
            chosen_part = lax.dynamic_slice_in_dim(chosen, first_row, block_size, 0)
            applied_part = lax.dynamic_slice_in_dim(applied, first_row, block_size, 0)
            cos_part = lax.dynamic_slice_in_dim(cos_all, first_row, block_size, 0)
            sin_part = lax.dynamic_slice_in_dim(sin_all, first_row, block_size, 0)
            return summed_up + return_block(
                template_flat, applied_part, cos_part, sin_part, chosen_part
            )

        summed_up = lax.fori_loop(
            0, block_count, returned, jnp.zeros((2, band_count, wave_count), jnp.float32)
        )
        return lax.psum(summed_up, "atom") + kinetic[None, None, :] * fields

    applied_once = apply_once(bands_in)
    applied_twice = apply_once(applied_once)
    return (applied_once, applied_twice)


def solution(mesh):
    in_specs = (
        P(None, None, "pw"),
        P(None, None, "pw"),
        P(("pw", "atom"), None),
        P(None, "pw"),
        P(),
        P(),
        P(),
        P(),
    )
    out_specs = (P(None, None, "pw"), P(None, None, "pw"))
    return jax.shard_map(
        per_device, mesh=mesh, in_specs=in_specs, out_specs=out_specs, check_vma=False
    )
```

profile of v0, /device:TPU:1, one launch (start us, length us, event | category | flops | bytes accessed | tf_op | source)
XLA Modules:
  0.0 1698.9 jit_solution(8377880044509035921)
XLA Ops:
  8.7 0.9 copy.40
  9.7 1.4 gather_fusion
  12.1 1.9 gather_fusion.2
  14.0 3.1 fusion.24
  17.4 25.3 %while.48 = (s32[]{:T(128)}, f32[8,32,2,64,8]{3,4,1,0,2:T(8,128)S(1)}, s32[8]{0:T(128)S(1)}, f32[256,2]{0,1:T(2,128)S(1)}, f32[256,512]{1,0:T(8,128)}, /*index=5...) while((s32[]{:T(128)}, ...), condition=%wide.region_1.2_spmd, body=%wide.region_0.1_spmd.sunk | while | flops 68517896 | bytes 4819139 | solution.py:114
  18.6 0.9 constant_dynamic-slice_fusion.22
  21.8 0.9 constant_dynamic-slice_fusion.22
  25.0 0.9 constant_dynamic-slice_fusion.22
  28.1 0.9 constant_dynamic-slice_fusion.22
  31.3 0.9 constant_dynamic-slice_fusion.22
  34.5 0.9 constant_dynamic-slice_fusion.22
  37.6 0.9 constant_dynamic-slice_fusion.22
  42.7 1.3 copy-done.4
  44.9 1.9 add_multiply_fusion.1
  46.9 224.9 %all-gather.3.cloned.1.call-done = bf16[64,4,8192]{2,1,0:T(4,128)(2,1)} async-done(((bf16[1,4,8192]{2,1,0:T(4,128)(2,1)}), bf16[64,4,8192]{2,1,0:T(4,128)(2,1)}) %all-gather.3.cloned.1.call-update) | async-done | bytes 4194320 | tf_op jit(solution)/shard_map/all_gather | solution.py:118
  271.8 13.4 reshape.268
  285.2 601.6 %all-reduce.3.cloned.1.call-done = f32[256,2,64,8]{2,3,0,1:T(8,128)} async-done(((f32[256,2,64,8]{2,3,0,1:T(8,128)}), f32[256,2,64,8]{2,3,0,1:T(8,128)}) %all-reduce.3.cloned.1.call-update) | async-done | bytes 1048592 | tf_op jit(solution)/shard_map/psum | solution.py:117
  886.7 8.6 fusion.6
  895.4 8.6 fusion.7
  904.0 6.6 fusion.21
  910.6 6.6 fusion.20
  917.4 16.8 while.50
  934.2 57.2 %psum.29 = f32[2,8,512]{2,1,0:T(8,128)S(1)} all-reduce(f32[2,8,512]{2,1,0:T(8,128)S(1)} %get-tuple-element.335), channel_id=1, replica_groups=mesh['pw'=64,'atom'=4] {'atom'}, use_global_device_ids=true, to_apply=%region_7.8 | all-reduce | flops 8192 | bytes 65536 | tf_op jit(solution)/shard_map/psum | solution.py:137
  991.6 25.3 %while.49 = (s32[]{:T(128)}, f32[8,32,2,64,8]{3,4,1,0,2:T(8,128)S(1)}, s32[8]{0:T(128)S(1)}, f32[256,2]{0,1:T(2,128)S(1)}, f32[256,512]{1,0:T(8,128)}, /*index=5...) while((s32[]{:T(128)}, ...), condition=%wide.region_9.10_spmd, body=%wide.region_8.9_spmd.sunk | while | flops 68517896 | bytes 4819139 | solution.py:114
  1017.0 1.3 copy-done.3
  1018.3 567.7 %all-reduce.5.cloned.1.call-done = f32[256,2,64,8]{2,3,0,1:T(8,128)} async-done(((f32[256,2,64,8]{2,3,0,1:T(8,128)}), f32[256,2,64,8]{2,3,0,1:T(8,128)}) %all-reduce.5.cloned.1.call-update) | async-done | bytes 1048592 | tf_op jit(solution)/shard_map/psum | solution.py:117
  1586.1 8.6 fusion.4
  1594.7 8.5 fusion.5
  1603.2 8.3 fusion.23
  1611.5 6.6 fusion.22
  1618.4 16.8 while.51
  1635.1 56.6 %psum.31 = f32[2,8,512]{2,1,0:T(8,128)S(1)} all-reduce(f32[2,8,512]{2,1,0:T(8,128)S(1)} %get-tuple-element.337), channel_id=1, replica_groups=mesh['pw'=64,'atom'=4] {'atom'}, use_global_device_ids=true, to_apply=%region_15.16 | all-reduce | flops 8192 | bytes 65536 | tf_op jit(solution)/shard_map/psum | solution.py:137
  (395 shorter events, 70.2 us)
Async XLA Ops:
  7.2 2.5 copy-start
  7.2 10.1 copy-start.8
  7.2 10.1 copy-start.2
  7.2 264.6 %all-gather.3.cloned.1.call-start = ((), (), s32[]{:S(2)}) async-start(), calls=%async_computation.2 | async-start | bytes 4259840 | tf_op jit(solution)/shard_map/all_gather | solution.py:118
  7.9 878.8 %all-reduce.3.cloned.1.call-start = ((), (), s32[]{:S(2)}) async-start(), calls=%async_computation | async-start | bytes 4194304 | tf_op jit(solution)/shard_map/psum | solution.py:117
  17.3 26.9 %copy-start.9 = (f32[3]{0:T(128)S(1)}, f32[3]{0:T(128)}, u32[]{:S(2)}) copy-start(f32[3]{0:T(128)} %param.23) | copy-start | bytes 40
  42.7 1.3 copy-start.4
  44.0 1542.0 %all-reduce.5.cloned.1.call-start = ((), (), s32[]{:S(2)}) async-start(), calls=%async_computation.1 | async-start | bytes 4194304 | tf_op jit(solution)/shard_map/psum | solution.py:117
  886.7 17.3 %copy-start.1 = (bf16[256,2,64,64]{3,2,1,0:T(8,128)(2,1)S(1)}, bf16[256,2,64,64]{3,2,1,0:T(8,128)(2,1)}, u32[]{:S(2)}) copy-start(bf16[256,2,64,64]{3,2,1,0:T(8,128)(2,1)} %reshape.268) | copy-start | bytes 12582916
  895.3 8.6 copy-start.5
  1016.9 1.3 copy-start.3
  1017.0 674.8 %copy-start.7 = (f32[2,8,512]{2,1,0:T(8,128)}, f32[2,8,512]{2,1,0:T(8,128)S(1)}, u32[]{:S(2)}) copy-start(f32[2,8,512]{2,1,0:T(8,128)S(1)} %get-tuple-element.947) | copy-start | bytes 98308
  1586.1 8.6 copy-start.6
  1586.1 25.4 %slice-start = ((s8[8388608]{0:T(1024)(128)(4,1)}), s8[4194304]{0:T(1024)(128)(4,1)S(1)}, s32[]{:S(2)}) async-start(s8[8388608]{0:T(1024)(128)(4,1)} %bitcast.282), calls=%async_computation.3 | async-start | bytes 8388608
  1594.7 16.8 slice-start.1
Sparse Core Ops, SparseCore 0:
  9.8 261.9 all-gather.2
  274.4 612.2 all-reduce.2
  1018.4 567.5 all-reduce.4
where the time goes:
time: 1700 us
  waiting for transfers between devices  1390 us (82%)
  blocking collectives  114 us (7%)
  local copies, waits for them, and re-layouts  73.1 us (4%)
  matrix products  71.7 us (4%)
  other arithmetic  18.1 us (1%)
    psum x2, waiting for transfers between devices, apply_once(): summed = lax.psum(coeffs, 'pw')  1170 us
    all_gather x1, waiting for transfers between devices, apply_once(): segment = lax.all_gather(potential, 'pw', axis=0, tiled=True)  225 us
    psum x2, blocking collectives, apply_once(): return lax.psum(summed_up, 'atom') + kinetic[None, None, :] * fields  114 us
    dot_general x8, matrix products, product(): jnp.einsum('alm,amb->alb', matrices, vectors, precision=lax.Precision.HIG...  62.5 us
  transfers between devices with their start and end apart: 3, of which 3 were waited for; matrix products, arithmetic and copies ran while one was open for 3% of the time, Pallas kernels for 0%

commit v1 on v0

--- a/solution.py
+++ b/solution.py
@@ -1,3 +1,4 @@
+import functools
 import math
 import jax
 import jax.numpy as jnp
@@ -5,6 +6,13 @@
 from jax.sharding import PartitionSpec as P
 
 full_turn = 2.0 * math.pi
+
+
+def _begin_stacks_all(message, peer_axis):
+    return lax.all_gather(message, peer_axis).sum(axis=0)
+
+
+_register_types = functools.partial(_begin_stacks_all, peer_axis="atom")
 
 
 def phases(miller_real, centres):
@@ -134,7 +142,7 @@
         summed_up = lax.fori_loop(
             0, block_count, returned, jnp.zeros((2, band_count, wave_count), jnp.float32)
         )
-        return lax.psum(summed_up, "atom") + kinetic[None, None, :] * fields
+        return _register_types(summed_up) + kinetic[None, None, :] * fields
 
     applied_once = apply_once(bands_in)
     applied_twice = apply_once(applied_once)

time: 1700 us -> 1690 us (level)
    psum x2 -> x0, blocking collectives: 114 us -> none  [apply_once(): return lax.psum(summed_up, 'atom') + kinetic[None, None, :] * fields]
    all_gather x0 -> x2, blocking collectives: none -> 102 us  [_begin_stacks_all(): return lax.all_gather(message, peer_axis).sum(axis=0)]
where the time goes in v1:
time: 1690 us
  waiting for transfers between devices  1390 us (82%)
  blocking collectives  102 us (6%)
  local copies, waits for them, and re-layouts  73.1 us (4%)
  matrix products  71.7 us (4%)
  other arithmetic  18.1 us (1%)
    psum x2, waiting for transfers between devices, apply_once(): summed = lax.psum(coeffs, 'pw')  1170 us
    all_gather x1, waiting for transfers between devices, apply_once(): segment = lax.all_gather(potential, 'pw', axis=0, tiled=True)  225 us
    all_gather x2, blocking collectives, _begin_stacks_all(): return lax.all_gather(message, peer_axis).sum(axis=0)  102 us
    dot_general x8, matrix products, product(): jnp.einsum('alm,amb->alb', matrices, vectors, precision=lax.Precision.HIG...  62.5 us
  transfers between devices with their start and end apart: 3, of which 3 were waited for; matrix products, arithmetic and copies ran while one was open for 3% of the time, Pallas kernels for 0%

profile of v1, /device:TPU:1, one launch (start us, length us, event | category | flops | bytes accessed | tf_op | source)
XLA Modules:
  0.0 1686.8 jit_solution(5782890927761317548)
XLA Ops:
  8.7 0.9 copy.40
  9.7 1.4 gather_fusion
  12.1 1.9 gather_fusion.2
  14.0 3.1 fusion.24
  17.4 25.3 %while.48 = (s32[]{:T(128)}, f32[8,32,2,64,8]{3,4,1,0,2:T(8,128)S(1)}, s32[8]{0:T(128)S(1)}, f32[256,2]{0,1:T(2,128)S(1)}, f32[256,512]{1,0:T(8,128)}, /*index=5...) while((s32[]{:T(128)}, ...), condition=%wide.region_1.2_spmd, body=%wide.region_0.1_spmd.sunk | while | flops 68517896 | bytes 4819139 | solution.py:122
  18.6 0.9 constant_dynamic-slice_fusion.22
  21.8 0.9 constant_dynamic-slice_fusion.22
  25.0 0.9 constant_dynamic-slice_fusion.22
  28.1 0.9 constant_dynamic-slice_fusion.22
  31.3 0.9 constant_dynamic-slice_fusion.22
  34.5 0.9 constant_dynamic-slice_fusion.22
  37.6 0.9 constant_dynamic-slice_fusion.22
  42.7 1.3 copy-done.3
  44.9 1.9 add_multiply_fusion.1
  46.9 224.9 %all-gather.5.cloned.1.call-done = bf16[64,4,8192]{2,1,0:T(4,128)(2,1)} async-done(((bf16[1,4,8192]{2,1,0:T(4,128)(2,1)}), bf16[64,4,8192]{2,1,0:T(4,128)(2,1)}) %all-gather.5.cloned.1.call-update) | async-done | bytes 4194320 | tf_op jit(solution)/shard_map/all_gather | solution.py:126
  271.8 13.4 reshape.268
  285.2 601.6 %all-reduce.3.cloned.1.call-done = f32[256,2,64,8]{2,3,0,1:T(8,128)} async-done(((f32[256,2,64,8]{2,3,0,1:T(8,128)}), f32[256,2,64,8]{2,3,0,1:T(8,128)}) %all-reduce.3.cloned.1.call-update) | async-done | bytes 1048592 | tf_op jit(solution)/shard_map/psum | solution.py:125
  886.7 8.6 fusion.6
  895.4 8.6 fusion.7
  904.0 6.6 fusion.21
  910.6 6.6 fusion.20
  917.4 16.8 while.50
  934.2 51.1 %all-gather = f32[8,8,512]{2,1,0:T(8,128)S(1)} all-gather(f32[2,8,512]{2,1,0:T(8,128)S(1)} %get-tuple-element.335), channel_id=2, replica_groups=mesh['pw'=64,'atom'=4] {'atom'}, dimensions={0}, use_global_device_ids=true | all-gather | bytes 163840 | tf_op jit(solution)/shard_map/all_gather | solution.py:12
  985.5 25.3 %while.49 = (s32[]{:T(128)}, f32[8,32,2,64,8]{3,4,1,0,2:T(8,128)S(1)}, s32[8]{0:T(128)S(1)}, f32[256,2]{0,1:T(2,128)S(1)}, f32[256,512]{1,0:T(8,128)}, /*index=5...) while((s32[]{:T(128)}, ...), condition=%wide.region_9.10_spmd, body=%wide.region_8.9_spmd.sunk | while | flops 68517896 | bytes 4819139 | solution.py:122
  1010.8 1.3 copy-done.4
  1012.2 567.5 %all-reduce.5.cloned.1.call-done = f32[256,2,64,8]{2,3,0,1:T(8,128)} async-done(((f32[256,2,64,8]{2,3,0,1:T(8,128)}), f32[256,2,64,8]{2,3,0,1:T(8,128)}) %all-reduce.5.cloned.1.call-update) | async-done | bytes 1048592 | tf_op jit(solution)/shard_map/psum | solution.py:125
  1579.7 8.6 fusion.4
  1588.4 8.5 fusion.5
  1596.8 8.3 fusion.23
  1605.2 6.6 fusion.22
  1612.0 16.8 while.51
  1628.8 50.8 %all-gather.1 = f32[8,8,512]{2,1,0:T(8,128)S(1)} all-gather(f32[2,8,512]{2,1,0:T(8,128)S(1)} %get-tuple-element.337), channel_id=3, replica_groups=mesh['pw'=64,'atom'=4] {'atom'}, dimensions={0}, use_global_device_ids=true | all-gather | bytes 163840 | tf_op jit(solution)/shard_map/all_gather | solution.py:12
  (397 shorter events, 70.3 us)
Async XLA Ops:
  7.2 2.5 copy-start
  7.2 10.1 copy-start.8
  7.2 10.1 copy-start.2
  7.2 264.6 %all-gather.5.cloned.1.call-start = ((), (), s32[]{:S(2)}) async-start(), calls=%async_computation.2 | async-start | bytes 4259840 | tf_op jit(solution)/shard_map/all_gather | solution.py:126
  7.9 878.8 %all-reduce.3.cloned.1.call-start = ((), (), s32[]{:S(2)}) async-start(), calls=%async_computation | async-start | bytes 4194304 | tf_op jit(solution)/shard_map/psum | solution.py:125
  17.3 26.9 %copy-start.9 = (f32[3]{0:T(128)S(1)}, f32[3]{0:T(128)}, u32[]{:S(2)}) copy-start(f32[3]{0:T(128)} %param.23) | copy-start | bytes 40
  42.7 1.3 copy-start.3
  44.0 1535.7 %all-reduce.5.cloned.1.call-start = ((), (), s32[]{:S(2)}) async-start(), calls=%async_computation.1 | async-start | bytes 4194304 | tf_op jit(solution)/shard_map/psum | solution.py:125
  886.7 17.3 %copy-start.1 = (bf16[256,2,64,64]{3,2,1,0:T(8,128)(2,1)S(1)}, bf16[256,2,64,64]{3,2,1,0:T(8,128)(2,1)}, u32[]{:S(2)}) copy-start(bf16[256,2,64,64]{3,2,1,0:T(8,128)(2,1)} %reshape.268) | copy-start | bytes 12582916
  895.3 8.6 copy-start.5
  1010.8 1.3 copy-start.4
  1010.8 668.8 %copy-start.7 = (f32[2,8,512]{2,1,0:T(8,128)}, f32[2,8,512]{2,1,0:T(8,128)S(1)}, u32[]{:S(2)}) copy-start(f32[2,8,512]{2,1,0:T(8,128)S(1)} %get-tuple-element.947) | copy-start | bytes 98308
  1579.7 8.6 copy-start.6
  1579.7 25.4 %slice-start = ((s8[8388608]{0:T(1024)(128)(4,1)}), s8[4194304]{0:T(1024)(128)(4,1)S(1)}, s32[]{:S(2)}) async-start(s8[8388608]{0:T(1024)(128)(4,1)} %bitcast.284), calls=%async_computation.3 | async-start | bytes 8388608
  1588.4 16.8 slice-start.1
Sparse Core Ops, SparseCore 0:
  9.8 261.9 all-gather.4
  274.4 612.2 all-reduce.2
  1012.3 567.3 all-reduce.4
